TPU v7x, 128 devices: a whole 4x4x4 slice. The times are simulated.
128 devices in a mesh: ctx: 16 (over y, z_hi, core), dp: 8 (over x, z_lo).
Axes of the slice: x: 4, y: 4, z: 4 (z_hi: 2, z_lo: 2; z = z_hi * 2 + z_lo), core: 2. Of those that a mesh axis runs over, the one named last changes fastest.
Arguments:
- tokens: bfloat16 [8, 4096, 16384], P('dp', 'ctx'), may hold values from -6 to 6
- queries: bfloat16 [8, 4096, 1024], P('dp', 'ctx'), may hold values from -200 to 200
- cotangent: bfloat16 [8, 4096, 1024], P('dp', 'ctx'), may hold values from -6 to 6
- latent_key: float32 [16384, 128], P(('ctx', 'dp')), may hold values from -1 to 1
- latent_value: float32 [16384, 128], P(('ctx', 'dp')), may hold values from -1 to 1
- lengths: int32 [8, 8], P('dp'), may hold values from 1 to 2048, 4096 in all within a row
- block_order: int32 [8, 32], P('dp'), may hold values from 0 to 31, each once within a row
Outputs:
- attn_out: bfloat16 [8, 4096, 1024], P('dp', 'ctx')
- query_grad: bfloat16 [8, 4096, 1024], P('dp', 'ctx')
- token_grad: bfloat16 [8, 4096, 16384], P('dp', 'ctx')
- key_weight_grad: float32 [16384, 128], P(('ctx', 'dp'))
- value_weight_grad: float32 [16384, 128], P(('ctx', 'dp'))
Inputs may be any that keep to these rules, and one draw needn't show every extreme that they name: Each row holds the lengths of the 8 documents packed into one sequence, in order; they sum to 4096 and the largest is exactly 2048. Each row is a permutation; stored block b of a sequence (rows b * 128 to (b + 1) * 128 - 1) holds the tokens at positions block_order[b] * 128 to block_order[b] * 128 + 127.
All inputs are finite; a program needn't handle non-finite values. Where the computation divides by a largest or mean magnitude, that divisor is 1e-20 or more.
Results may differ from a plain program's by a relative error of at most 0.02.
The roundings to bfloat16 on the way count: a program that leaves them out, or rounds other values in their place, can miss the bound.
Values may be sent and summed in bfloat16 or wider, within the bound.
No kernel may reach another device: no remote copies, remote signals or barrier semaphores. Data moves between devices by JAX's collectives and lax.ppermute only.
A program may use at most 128 MiB of HBM per device.

v0:
```python
import jax
import jax.numpy as jnp
from jax import lax
from jax.sharding import Mesh
from jax.sharding import PartitionSpec as P

CTX = ("ctx_0", "ctx_1", "ctx_2")
CTX_DP = ("ctx_0", "ctx_1", "ctx_2", "dp_0", "dp_1")
DP = ("dp_0", "dp_1")
EPSILON = 1e-05
NEGATIVE = -1e30


def over_axes(value, axes):
    for axis in axes:
        value = lax.psum(value, axis)
    return value


def in_one_piece(arrays, axis, dim, along):
    both = jnp.concatenate(arrays, axis=along)
    result, at, done = (lax.all_gather(both, axis, axis=dim, tiled=True), 0, [])
    for a in arrays:
        done.append(lax.slice_in_dim(result, at, at + a.shape[along], axis=along))
        at += a.shape[along]
    return tuple(done)


def levels(ratio):
    return jnp.where(ratio >= 0.5, 1.0, jnp.where(ratio <= -0.5, -1.0, 0.0)).astype(jnp.float32)


def over_blocks(advance, state_now, key_rows, value_rows):
    row_total = key_rows.shape[0]
    width_rows = 512
    block_count = row_total // width_rows
    key_blocks = key_rows.reshape(block_count, width_rows, key_rows.shape[1])
    value_blocks = value_rows.reshape(block_count, width_rows, value_rows.shape[1])

    def turn_once(carried, block_item):
        key_block, value_block, number = block_item
        return (advance(carried, key_block, value_block, number * width_rows), None)

    state_now, _ = lax.scan(
        turn_once, state_now, (key_blocks, value_blocks, jnp.arange(block_count, dtype=jnp.int32))
    )
    return state_now


def body(tokens, queries, cotangent, latent_key, latent_value, lengths, block_order):
    token_rows = tokens[0]
    rows_here = token_rows.shape[0]
    head_size = latent_key.shape[1]
    head_count = queries.shape[2] // head_size
    scale_factor = head_size ** (-0.5)
    block_rows = rows_here // 2
    lengths_row = lengths[0]
    order_row = block_order[0]
    block_ids = jnp.arange(order_row.shape[0], dtype=jnp.int32)
    doc_starts = jnp.cumsum(lengths_row, dtype=jnp.int32) - lengths_row

    def positions(stored):
        owner = jnp.sum(
            jnp.where((stored // block_rows)[:, None] == block_ids[None, :], order_row[None, :], 0),
            axis=1,
        )
        return owner * block_rows + stored % block_rows

    def documents(position):
        return jnp.sum((position[:, None] >= doc_starts[None, :]).astype(jnp.int32), axis=1)

    query_pos = positions(lax.axis_index(CTX) * rows_here + jnp.arange(rows_here, dtype=jnp.int32))
    query_doc = documents(query_pos)

    def visibility(first_row, row_total):
        key_pos = positions(first_row + jnp.arange(row_total, dtype=jnp.int32))
        key_doc = documents(key_pos)
        return (key_pos[None, :] <= query_pos[:, None]) & (key_doc[None, :] == query_doc[:, None])

    entry_count = latent_key.shape[0] * lax.axis_size(CTX_DP) * head_size
    magnitudes = (
        over_axes(jnp.sum(jnp.abs(latent_key)), CTX_DP),
        over_axes(jnp.sum(jnp.abs(latent_value)), CTX_DP),
    )
    key_scale = magnitudes[0] / entry_count + EPSILON
    value_scale = magnitudes[1] / entry_count + EPSILON
    local_rows = jnp.concatenate(
        [
            (key_scale * levels(latent_key / key_scale)).astype(jnp.bfloat16),
            (value_scale * levels(latent_value / value_scale)).astype(jnp.bfloat16),
        ],
        axis=1,
    )
    both = lax.all_gather(local_rows, CTX_DP, axis=0, tiled=True)
    projected = jnp.dot(token_rows, both, preferred_element_type=jnp.float32).astype(jnp.bfloat16)
    key_pair = (projected[:, :head_size][None], projected[:, head_size:][None])
    query_heads = queries[0].reshape(rows_here, head_count, head_size)
    cot_heads = cotangent[0].reshape(rows_here, head_count, head_size)

    def forward_block(state_now, key_block, value_block, first_row):
        best, total, accum = state_now
        scores = (
            jnp.einsum("thd,sd->hts", query_heads, key_block, preferred_element_type=jnp.float32)
            * scale_factor
        )
        visible = visibility(first_row, key_block.shape[0])
        scores = jnp.where(visible[None], scores, NEGATIVE)
        new_best = jnp.maximum(best, jnp.max(scores, axis=2))
        weights = jnp.where(visible[None], jnp.exp(scores - new_best[:, :, None]), 0.0)
        shrink = jnp.exp(best - new_best)
        total = total * shrink + jnp.sum(weights, axis=2)
        accum = accum * shrink.T[:, :, None] + jnp.einsum(
            "hts,sd->thd",
            weights.astype(jnp.bfloat16),
            value_block,
            preferred_element_type=jnp.float32,
        )
        return (new_best, total, accum)

    start_state = (
        jnp.full((head_count, rows_here), NEGATIVE, jnp.float32),
        jnp.zeros((head_count, rows_here), jnp.float32),
        jnp.zeros((rows_here, head_count, head_size), jnp.float32),
    )
    shard_part = in_one_piece((key_pair[0], key_pair[1]), CTX, 1, 0)
    state_final = over_blocks(forward_block, start_state, shard_part[0][0], shard_part[1][0])
    all_keys, all_values = in_one_piece((key_pair[0], key_pair[1]), CTX, 1, 0)
    best, total, accum = state_final
    log_total = best + jnp.log(total)
    mixed = (accum / total.T[:, :, None]).astype(jnp.bfloat16)
    expected = jnp.sum(cot_heads.astype(jnp.float32) * mixed.astype(jnp.float32), axis=2).T

    def backward_block(query_acc, key_block, value_block, first_row):
        scores = (
            jnp.einsum("thd,sd->hts", query_heads, key_block, preferred_element_type=jnp.float32)
            * scale_factor
        )
        visible = visibility(first_row, key_block.shape[0])
        probability = jnp.where(visible[None], jnp.exp(scores - log_total[:, :, None]), 0.0)
        prob_grad = jnp.einsum(
            "thd,sd->hts", cot_heads, value_block, preferred_element_type=jnp.float32
        )
        score_grad = (probability * (prob_grad - expected[:, :, None])).astype(jnp.bfloat16)
        query_acc = (
            query_acc
            + jnp.einsum("hts,sd->thd", score_grad, key_block, preferred_element_type=jnp.float32)
            * scale_factor
        )
        key_part = (
            jnp.einsum("hts,thd->sd", score_grad, query_heads, preferred_element_type=jnp.float32)
            * scale_factor
        )
        value_part = jnp.einsum(
            "hts,thd->sd",
            probability.astype(jnp.bfloat16),
            cot_heads,
            preferred_element_type=jnp.float32,
        )
        return (query_acc, jnp.concatenate([key_part, value_part], axis=1))

    key_all = all_keys[0]
    value_all = all_values[0]
    total_rows = key_all.shape[0]
    width_rows = 512
    block_count = total_rows // width_rows

    def backward_turn(query_acc, block_item):
        key_block, value_block, number = block_item
        return backward_block(query_acc, key_block, value_block, number * width_rows)

    query_acc, key_terms = lax.scan(
        backward_turn,
        jnp.zeros((rows_here, head_count, head_size), jnp.float32),
        (
            key_all.reshape(block_count, width_rows, head_size),
            value_all.reshape(block_count, width_rows, head_size),
            jnp.arange(block_count, dtype=jnp.int32),
        ),
    )
    key_terms = key_terms.reshape(total_rows, 2 * head_size)
    grads_kv = lax.psum_scatter(key_terms, CTX, scatter_dimension=0, tiled=True).astype(
        jnp.bfloat16
    )
    token_grad = lax.dot_general(
        grads_kv, both, (((1,), (1,)), ((), ())), preferred_element_type=jnp.float32
    ).astype(jnp.bfloat16)
    columns_all = lax.all_to_all(token_rows, CTX_DP, split_axis=1, concat_axis=0, tiled=True)
    summed = lax.dot_general(
        columns_all,
        lax.all_gather(grads_kv, CTX_DP, axis=0, tiled=True),
        (((0,), (0,)), ((), ())),
        preferred_element_type=jnp.float32,
    )
    key_weight_grad = summed[:, :head_size]
    value_weight_grad = summed[:, head_size:]
    attn_out = mixed.reshape(rows_here, head_count * head_size)[None]
    query_grad = query_acc.astype(jnp.bfloat16).reshape(rows_here, head_count * head_size)[None]
    return (attn_out, query_grad, token_grad[None], key_weight_grad, value_weight_grad)


def solution(mesh):
    torus = Mesh(mesh.devices.reshape(4, 2, 2, 4, 2), ("ctx_0", "ctx_1", "ctx_2", "dp_0", "dp_1"))
    in_specs = (
        P(DP, CTX, None),
        P(DP, CTX, None),
        P(DP, CTX, None),
        P(CTX_DP, None),
        P(CTX_DP, None),
        P(DP, None),
        P(DP, None),
    )
    out_specs = (
        P(DP, CTX, None),
        P(DP, CTX, None),
        P(DP, CTX, None),
        P(CTX_DP, None),
        P(CTX_DP, None),
    )
    return jax.shard_map(body, mesh=torus, in_specs=in_specs, out_specs=out_specs, check_vma=False)
```

profile of v0, /device:TPU:73, one launch (start us, length us, event | category | flops | bytes accessed | tf_op | source)
XLA Modules:
  0.0 1085.5 jit_solution(9353580749844137275)
XLA Ops:
  8.7 7.3 all-reduce.1
  16.0 5.9 all-reduce.4
  21.9 6.6 all-reduce.3
  28.5 9.1 all-reduce
  37.6 4.4 all-reduce.2
  45.8 314.5 %all-gather.4.cloned.1.call-done = bf16[16384,256]{1,0:T(8,128)(2,1)} async-done(((bf16[128,256]{1,0:T(8,128)(2,1)}), bf16[16384,256]{1,0:T(8,128)(2,1)}) %all-gather.4.cloned.1.call-update) | async-done | bytes 8388624 | tf_op jit(solution)/shard_map/all_gather | solution.py:94
  360.3 8.1 fusion.68
  371.4 44.9 %all-gather.6.cloned.1.call-done = bf16[2,4096,128]{1,2,0:T(8,128)(2,1)} async-done(((bf16[2,256,128]{1,2,0:T(8,128)(2,1)}), bf16[2,4096,128]{1,2,0:T(8,128)(2,1)}) %all-gather.6.cloned.1.call-update) | async-done | bytes 2097168 | tf_op jit(solution)/shard_map/all_gather | solution.py:22
  416.3 2.7 fusion.74
  424.7 62.8 %while.32 = (s32[]{:T(128)}, f32[8,256]{1,0:T(8,128)S(1)}, f32[8,256]{1,0:T(8,128)S(1)}, f32[256,8,128]{0,2,1:T(8,128)}, s32[8]{0:T(128)S(1)}, /*index=5*/s32[1,...) while((s32[]{:T(128)}, f32[8,256]{1,0:T(8,128)S(1)}, ...), condition=%wide.region_20.21_spmd.clone, body=%wide.region_15.20_spmd.clone.sunk | while | flops 551770112 | bytes 24531360 | solution.py:44
  429.2 2.4 fusion.121
  437.0 2.4 fusion.121
  444.9 2.4 fusion.121
  452.7 2.4 fusion.121
  460.6 2.4 fusion.121
  468.4 2.4 fusion.121
  489.7 80.0 %while.33 = (s32[]{:T(128)}, f32[256,8,128]{0,2,1:T(8,128)S(1)}, f32[8,512,256]{2,1,0:T(8,128)}, bf16[8,512,128]{2,1,0:T(8,128)(2,1)}, s32[8]{0:T(128)S(1)}, /*i...) while((s32[]{:T(128)}, f32[256,8,128]{0,2,1:T(8,128)S(1)}, ...), condition=%wide.region_25.26_spmd.clone, body=%wide.region_22.25_spmd.clone.sunk | while | flops 1354115072 | bytes 27570560 | solution.py:171
  569.8 77.3 %reduce-scatter.2.cloned.1.call-done = f32[256,256]{1,0:T(8,128)} async-done(((f32[4096,256]{1,0:T(8,128)}), f32[256,256]{1,0:T(8,128)}) %reduce-scatter.2.cloned.1.call-update) | async-done | bytes 262160 | tf_op jit(solution)/shard_map/reduce_scatter | solution.py:181
  648.7 11.9 %copy.87 = bf16[1,256,16384]{1,2,0:T(8,128)(2,1)} copy(bf16[1,256,16384]{2,1,0:T(8,128)(2,1)} %param.11) | data formatting | bytes 16777216 | tf_op args[0]
  660.6 114.3 %all_to_all.19 = bf16[256,128,128]{0,2,1:T(8,128)(2,1)} all-to-all(bf16[256,128,128]{0,2,1:T(8,128)(2,1)} %bitcast.195), channel_id=1, replica_groups=mesh['ctx_0'=4,'ctx_1'=2,'ctx_2'=2,'dp_0'=4,'dp_1'=2] {'ctx_0','ctx_1','..., dimensions={1} | all-to-all | bytes 16777216 | tf_op jit(solution)/shard_map/all_to_all | solution.py:187
  775.0 12.0 %copy.88 = bf16[128,256,128]{2,1,0:T(8,128)(2,1)} copy(bf16[128,256,128]{1,2,0:T(8,128)(2,1)} %bitcast.194) | data formatting | bytes 16777216 | tf_op jit(solution)/shard_map/all_to_all | solution.py:187
  789.0 9.2 fusion.62
  798.2 268.7 %all-gather.8.cloned.1.call-done = bf16[32768,256]{1,0:T(8,128)(2,1)} async-done(((bf16[256,256]{1,0:T(8,128)(2,1)}), bf16[32768,256]{1,0:T(8,128)(2,1)}) %all-gather.8.cloned.1.call-update) | async-done | bytes 16777232 | tf_op jit(solution)/shard_map/all_gather | solution.py:190
  1066.9 10.6 convolution_bitcast_fusion.1
  (292 shorter events, 136.9 us)
Async XLA Ops:
  7.2 353.1 %all-gather.4.cloned.1.call-start = ((), (), s32[]{:S(2)}) async-start(), calls=%async_computation.2 | async-start | bytes 8454144 | tf_op jit(solution)/shard_map/all_gather | solution.py:94
  45.7 323.8 %copy-start.8 = (s32[1,8]{1,0:T(1,128)S(1)}, s32[1,8]{1,0:T(1,128)}, u32[]{:S(2)}) copy-start(s32[1,8]{1,0:T(1,128)} %param.16) | copy-start | bytes 100
  45.7 323.9 %copy-start.5 = (bf16[1,256,1024]{2,1,0:T(8,128)(2,1)S(1)}, bf16[1,256,1024]{2,1,0:T(8,128)(2,1)}, u32[]{:S(2)}) copy-start(bf16[1,256,1024]{2,1,0:T(8,128)(2,1)} %param.12) | copy-start | bytes 1572868
  45.7 324.4 %copy-start.6 = (bf16[1,256,1024]{2,1,0:T(8,128)(2,1)S(1)}, bf16[1,256,1024]{2,1,0:T(8,128)(2,1)}, u32[]{:S(2)}) copy-start(bf16[1,256,1024]{2,1,0:T(8,128)(2,1)} %param.13) | copy-start | bytes 1572868
  45.7 325.4 %copy-start.7 = (s32[1,32]{1,0:T(1,128)S(1)}, s32[1,32]{1,0:T(1,128)}, u32[]{:S(2)}) copy-start(s32[1,32]{1,0:T(1,128)} %param.17) | copy-start | bytes 388
  45.7 370.6 %all-gather.6.cloned.1.call-start = ((), (), s32[]{:S(2)}) async-start(), calls=%async_computation.3 | async-start | bytes 2228224 | tf_op jit(solution)/shard_map/all_gather | solution.py:22
  369.2 277.9 %reduce-scatter.2.cloned.1.call-start = ((), (), s32[]{:S(2)}) async-start(), calls=%async_computation.4 | async-start | bytes 4456448 | tf_op jit(solution)/shard_map/reduce_scatter | solution.py:181
  424.7 62.8 %copy-start = (bf16[1,256,1024]{1,2,0:T(8,128)(2,1)S(1)}, bf16[1,256,1024]{1,2,0:T(8,128)(2,1)}, u32[]{:S(2)}) copy-start(bf16[1,256,1024]{1,2,0:T(8,128)(2,1)} %copy.82) | copy-start | bytes 1572868
  426.3 2.8 copy-start.3
  431.6 1.0 copy-start.4
  434.2 2.8 copy-start.3
  439.4 1.0 copy-start.4
  442.1 2.8 copy-start.3
  447.3 1.0 copy-start.4
  449.9 2.8 copy-start.3
  455.1 1.0 copy-start.4
  457.7 2.8 copy-start.3
  463.0 1.0 copy-start.4
  465.6 2.8 copy-start.3
  473.4 2.8 copy-start.3
  481.3 2.8 copy-start.3
  569.7 497.2 %all-gather.8.cloned.1.call-start = ((), (), s32[]{:S(2)}) async-start(), calls=%async_computation.5 | async-start | bytes 16908288 | tf_op jit(solution)/shard_map/all_gather | solution.py:190
  775.0 12.0 %copy-start.1 = (bf16[256,8,128]{0,2,1:T(8,128)(2,1)S(1)}, bf16[256,8,128]{0,2,1:T(8,128)(2,1)}, u32[]{:S(2)}) copy-start(bf16[256,8,128]{0,2,1:T(8,128)(2,1)} %get-tuple-element.642) | copy-start | bytes 1572868
  775.0 14.1 %copy-start.2 = (bf16[256,256]{1,0:T(8,128)(2,1)S(1)}, bf16[256,256]{1,0:T(8,128)(2,1)}, u32[]{:S(2)}) copy-start(bf16[256,256]{1,0:T(8,128)(2,1)} %convert_element_type.72) | copy-start | bytes 393220
  (3 other events, 2.9 us)
Sparse Core Ops, SparseCore 0:
  45.8 314.4 all-gather.3
  369.3 46.9 all-gather.5
  569.9 77.1 reduce-scatter.1
  648.8 418.0 all-gather.7
where the time goes:
time: 1090 us
  waiting for transfers between devices  705 us (65%)
  blocking collectives  148 us (14%)
  matrix products  119 us (11%)
  local copies, waits for them, and re-layouts  62.5 us (6%)
  other arithmetic  23.8 us (2%)
  between operations  15.3 us (1%)
  loops' own time  11.6 us (1%)
    all_gather x1, waiting for transfers between devices, body(): both = lax.all_gather(local_rows, CTX_DP, axis=0, tiled=True)  315 us
    all_gather x1, waiting for transfers between devices, body(): lax.all_gather(grads_kv, CTX_DP, axis=0, tiled=True)  269 us
    all_to_all x1, blocking collectives, body(): lax.all_to_all(token_rows, CTX_DP, split_axis=1, concat_axis=0, tiled=True)  114 us
    reduce_scatter x1, waiting for transfers between devices, body(): lax.psum_scatter(key_terms, CTX, scatter_dimension=0, tiled=True)  77.3 us
    all_gather x1, waiting for transfers between devices, in_one_piece(): result, at, done = (lax.all_gather(both, axis, axis=dim, tiled=True), 0, [])  44.9 us
    psum x5, blocking collectives, over_axes(): value = lax.psum(value, axis)  33.3 us
  transfers between devices with their start and end apart: 4, of which 4 were waited for; matrix products, arithmetic and copies ran while one was open for 3% of the time, Pallas kernels for 0%

commit v1 on v0

--- a/solution.py
+++ b/solution.py
@@ -91,7 +91,15 @@
         ],
         axis=1,
     )
-    both = lax.all_gather(local_rows, CTX_DP, axis=0, tiled=True)
+
+    def refer_the_levels_all(target):
+        b_next = tuple((target for _ in range(lax.axis_size(CTX_DP))))
+        s_next = jnp.stack(b_next, axis=0)
+        d_next = lax.all_to_all(s_next, axis_name=CTX_DP, split_axis=0, concat_axis=0)
+        prior = jnp.concatenate(d_next, 0)
+        return prior
+
+    both = refer_the_levels_all(local_rows)
     projected = jnp.dot(token_rows, both, preferred_element_type=jnp.float32).astype(jnp.bfloat16)
     key_pair = (projected[:, :head_size][None], projected[:, head_size:][None])
     query_heads = queries[0].reshape(rows_here, head_count, head_size)

time: 1090 us -> 879 us (0.81)
  waiting for transfers between devices: 705 us -> 390 us
  blocking collectives: 148 us -> 252 us
    all_gather x1 -> x0, waiting for transfers between devices: 315 us -> none  [body(): both = lax.all_gather(local_rows, CTX_DP, axis=0, tiled=True)]
    all_to_all x0 -> x1, blocking collectives: none -> 105 us  [refer_the_levels_all(): lax.all_to_all(s_next, axis_name=CTX_DP, split_axis=0, concat_axis=0)]
  transfers between devices with their start and end apart: 4 -> 3, of which waited for: 4 -> 3; matrix products, arithmetic and copies ran while one was open for 3% -> 4% of each run, Pallas kernels for 0% -> 0%
where the time goes in v1:
time: 879 us; the launch traced here: 876 us
  waiting for transfers between devices  390 us (44%)
  blocking collectives  252 us (29%)
  matrix products  120 us (14%)
  local copies, waits for them, and re-layouts  63.5 us (7%)
  other arithmetic  23.2 us (3%)
  between operations  15.2 us (2%)
  loops' own time  11.6 us (1%)
    all_gather x1, waiting for transfers between devices, body(): lax.all_gather(grads_kv, CTX_DP, axis=0, tiled=True)  267 us
    all_to_all x1, blocking collectives, body(): lax.all_to_all(token_rows, CTX_DP, split_axis=1, concat_axis=0, tiled=True)  114 us
    all_to_all x1, blocking collectives, refer_the_levels_all(): lax.all_to_all(s_next, axis_name=CTX_DP, split_axis=0, concat_axis=0)  105 us
    reduce_scatter x1, waiting for transfers between devices, body(): lax.psum_scatter(key_terms, CTX, scatter_dimension=0, tiled=True)  77.3 us
    all_gather x1, waiting for transfers between devices, in_one_piece(): result, at, done = (lax.all_gather(both, axis, axis=dim, tiled=True), 0, [])  45.8 us
    psum x5, blocking collectives, over_axes(): value = lax.psum(value, axis)  33.3 us
    unnamed x26, local copies, waits for them, and re-layouts  20.6 us
    dot_general x8, matrix products, forward_block(): jnp.einsum('hts,sd->thd', weights.astype(jnp.bfloat16), value_block, pref...  19 us
  transfers between devices with their start and end apart: 3, of which 3 were waited for; matrix products, arithmetic and copies ran while one was open for 4% of the time, Pallas kernels for 0%

profile of v1, /device:TPU:73, one launch (start us, length us, event | category | flops | bytes accessed | tf_op | source)
XLA Modules:
  0.0 876.3 jit_solution(229647358590829265)
XLA Ops:
  8.7 7.3 all-reduce.1
  16.0 5.9 all-reduce.4
  21.9 6.6 all-reduce.3
  28.5 9.1 %all-reduce = (f32[]{:T(128)}, f32[]{:T(128)}) all-reduce(f32[]{:T(128)} %get-tuple-element.635, f32[]{:T(128)} %get-tuple-element.636), channel_id=1, replica_groups=mesh['ctx_0'=4,'ctx_1'=2,'ctx_2'=2,'dp_0'=4,'dp_1'=2] {'dp_0'}, use_global_device_ids=true, to_apply=%region_10.11 | all-reduce | flops 2 | bytes 16 | tf_op jit(solution)/shard_map/psum | solution.py:16
  37.6 4.4 all-reduce.2
  46.1 105.0 %all_to_all.24 = bf16[128,128,256]{2,1,0:T(8,128)(2,1)S(1)} all-to-all(bf16[128,128,256]{2,1,0:T(8,128)(2,1)S(1)} %stack.2), channel_id=1, replica_groups=mesh['ctx_0'=4,'ctx_1'=2,'ctx_2'=2,'dp_0'=4,'dp_1'=2] {'ctx_0','ctx_1','..., dimensions={0} | all-to-all | bytes 16777216 | tf_op jit(solution)/shard_map/all_to_all | solution.py:98
  151.1 9.1 %fusion.68 = bf16[256,256]{0,1:T(8,128)(2,1)S(1)} fusion(bf16[16384,256]{1,0:T(8,128)(2,1)S(1)} %bitcast.195, bf16[1,256,16384]{2,1,0:T(8,128)(2,1)} %param.11), kind=kOutput, calls=%fused_computation.91 | convolution fusion | flops 2147549184 | bytes 16908288 | tf_op jit(solution)/shard_map/dot_general | solution.py:103
  163.1 45.8 %all-gather.3.cloned.1.call-done = bf16[2,4096,128]{1,2,0:T(8,128)(2,1)} async-done(((bf16[2,256,128]{1,2,0:T(8,128)(2,1)}), bf16[2,4096,128]{1,2,0:T(8,128)(2,1)}) %all-gather.3.cloned.1.call-update) | async-done | bytes 2097168 | tf_op jit(solution)/shard_map/all_gather | solution.py:22
  208.9 2.7 fusion.74
  217.3 62.8 %while.32 = (s32[]{:T(128)}, f32[8,256]{1,0:T(8,128)S(1)}, f32[8,256]{1,0:T(8,128)S(1)}, f32[256,8,128]{0,2,1:T(8,128)}, s32[8]{0:T(128)S(1)}, /*index=5*/s32[1,...) while((s32[]{:T(128)}, f32[8,256]{1,0:T(8,128)S(1)}, ...), condition=%wide.region_20.21_spmd.clone, body=%wide.region_15.20_spmd.clone.sunk | while | flops 551770112 | bytes 24531360 | solution.py:44
  221.8 2.4 fusion.121
  229.6 2.4 fusion.121
  237.5 2.4 fusion.121
  245.3 2.4 fusion.121
  253.1 2.4 fusion.121
  261.0 2.4 fusion.121
  282.3 80.0 %while.33 = (s32[]{:T(128)}, f32[256,8,128]{0,2,1:T(8,128)S(1)}, f32[8,512,256]{2,1,0:T(8,128)}, bf16[8,512,128]{2,1,0:T(8,128)(2,1)}, s32[8]{0:T(128)S(1)}, /*i...) while((s32[]{:T(128)}, f32[256,8,128]{0,2,1:T(8,128)S(1)}, ...), condition=%wide.region_25.26_spmd.clone, body=%wide.region_22.25_spmd.clone.sunk | while | flops 1354115072 | bytes 27570560 | solution.py:179
  362.4 77.3 %reduce-scatter.2.cloned.1.call-done = f32[256,256]{1,0:T(8,128)} async-done(((f32[4096,256]{1,0:T(8,128)}), f32[256,256]{1,0:T(8,128)}) %reduce-scatter.2.cloned.1.call-update) | async-done | bytes 262160 | tf_op jit(solution)/shard_map/reduce_scatter | solution.py:189
  441.2 11.9 %copy.87 = bf16[1,256,16384]{1,2,0:T(8,128)(2,1)} copy(bf16[1,256,16384]{2,1,0:T(8,128)(2,1)} %param.11) | data formatting | bytes 16777216 | tf_op args[0]
  453.2 114.2 %all_to_all.25 = bf16[256,128,128]{0,2,1:T(8,128)(2,1)} all-to-all(bf16[256,128,128]{0,2,1:T(8,128)(2,1)} %bitcast.198), channel_id=1, replica_groups=mesh['ctx_0'=4,'ctx_1'=2,'ctx_2'=2,'dp_0'=4,'dp_1'=2] {'ctx_0','ctx_1','..., dimensions={1} | all-to-all | bytes 16777216 | tf_op jit(solution)/shard_map/all_to_all | solution.py:195
  567.4 12.0 %copy.88 = bf16[128,256,128]{2,1,0:T(8,128)(2,1)} copy(bf16[128,256,128]{1,2,0:T(8,128)(2,1)} %bitcast.197) | data formatting | bytes 16777216 | tf_op jit(solution)/shard_map/all_to_all | solution.py:195
  581.4 9.2 %fusion.62 = bf16[1,256,16384]{2,1,0:T(8,128)(2,1)} fusion(bf16[256,256]{1,0:T(8,128)(2,1)S(1)} %copy-done.3, bf16[16384,256]{1,0:T(8,128)(2,1)} %bitcast.196), kind=kOutput, calls=%fused_computation.87 | convolution fusion | flops 2151677952 | bytes 16908288 | tf_op jit(solution)/shard_map/dot_general | solution.py:192
  590.6 267.1 %all-gather.5.cloned.1.call-done = bf16[32768,256]{1,0:T(8,128)(2,1)} async-done(((bf16[256,256]{1,0:T(8,128)(2,1)}), bf16[32768,256]{1,0:T(8,128)(2,1)}) %all-gather.5.cloned.1.call-update) | async-done | bytes 16777232 | tf_op jit(solution)/shard_map/all_gather | solution.py:198
  857.7 10.6 %convolution_bitcast_fusion.1 = f32[128,256]{0,1:T(8,128)S(1)} fusion(bf16[32768,256]{1,0:T(8,128)(2,1)} %all-gather.5.cloned.1.call-done, bf16[32768,128]{1,0:T(8,128)(2,1)} %bitcast.194), kind=kOutput, calls=%fused_computation.92 | convolution fusion | flops 2147483648 | bytes 25296896 | tf_op jit(solution)/shard_map/dot_general | solution.py:196
  (293 shorter events, 137.2 us)
Async XLA Ops:
  7.2 201.7 %all-gather.3.cloned.1.call-start = ((), (), s32[]{:S(2)}) async-start(), calls=%async_computation.3 | async-start | bytes 2228224 | tf_op jit(solution)/shard_map/all_gather | solution.py:22
  151.0 9.1 %copy-start = (bf16[128,128,256]{2,1,0:T(8,128)(2,1)}, bf16[128,128,256]{2,1,0:T(8,128)(2,1)S(1)}, u32[]{:S(2)}) copy-start(bf16[128,128,256]{2,1,0:T(8,128)(2,1)S(1)} %all_to_all.24) | copy-start | bytes 25165828
  151.1 10.1 %copy-start.9 = (s32[1,8]{1,0:T(1,128)S(1)}, s32[1,8]{1,0:T(1,128)}, u32[]{:S(2)}) copy-start(s32[1,8]{1,0:T(1,128)} %param.16) | copy-start | bytes 100
  151.1 10.3 %copy-start.6 = (bf16[1,256,1024]{2,1,0:T(8,128)(2,1)S(1)}, bf16[1,256,1024]{2,1,0:T(8,128)(2,1)}, u32[]{:S(2)}) copy-start(bf16[1,256,1024]{2,1,0:T(8,128)(2,1)} %param.12) | copy-start | bytes 1572868
  151.1 10.8 %copy-start.7 = (bf16[1,256,1024]{2,1,0:T(8,128)(2,1)S(1)}, bf16[1,256,1024]{2,1,0:T(8,128)(2,1)}, u32[]{:S(2)}) copy-start(bf16[1,256,1024]{2,1,0:T(8,128)(2,1)} %param.13) | copy-start | bytes 1572868
  151.1 11.8 %copy-start.8 = (s32[1,32]{1,0:T(1,128)S(1)}, s32[1,32]{1,0:T(1,128)}, u32[]{:S(2)}) copy-start(s32[1,32]{1,0:T(1,128)} %param.17) | copy-start | bytes 388
  160.9 278.8 %reduce-scatter.2.cloned.1.call-start = ((), (), s32[]{:S(2)}) async-start(), calls=%async_computation.4 | async-start | bytes 4456448 | tf_op jit(solution)/shard_map/reduce_scatter | solution.py:189
  217.3 62.8 %copy-start.1 = (bf16[1,256,1024]{1,2,0:T(8,128)(2,1)S(1)}, bf16[1,256,1024]{1,2,0:T(8,128)(2,1)}, u32[]{:S(2)}) copy-start(bf16[1,256,1024]{1,2,0:T(8,128)(2,1)} %copy.82) | copy-start | bytes 1572868
  218.9 2.8 copy-start.4
  224.1 1.0 copy-start.5
  226.8 2.8 copy-start.4
  232.0 1.0 copy-start.5
  234.6 2.8 copy-start.4
  239.8 1.0 copy-start.5
  242.5 2.8 copy-start.4
  247.7 1.0 copy-start.5
  250.3 2.8 copy-start.4
  255.5 1.0 copy-start.5
  258.2 2.8 copy-start.4
  266.0 2.8 copy-start.4
  273.9 2.8 copy-start.4
  362.3 495.4 %all-gather.5.cloned.1.call-start = ((), (), s32[]{:S(2)}) async-start(), calls=%async_computation.5 | async-start | bytes 16908288 | tf_op jit(solution)/shard_map/all_gather | solution.py:198
  567.4 12.0 %copy-start.2 = (bf16[256,8,128]{0,2,1:T(8,128)(2,1)S(1)}, bf16[256,8,128]{0,2,1:T(8,128)(2,1)}, u32[]{:S(2)}) copy-start(bf16[256,8,128]{0,2,1:T(8,128)(2,1)} %get-tuple-element.642) | copy-start | bytes 1572868
  567.4 14.1 %copy-start.3 = (bf16[256,256]{1,0:T(8,128)(2,1)S(1)}, bf16[256,256]{1,0:T(8,128)(2,1)}, u32[]{:S(2)}) copy-start(bf16[256,256]{1,0:T(8,128)(2,1)} %convert_element_type.72) | copy-start | bytes 393220
  (3 other events, 2.9 us)
Sparse Core Ops, SparseCore 0:
  161.0 47.8 all-gather.2
  362.4 77.1 reduce-scatter.1
  441.4 416.2 all-gather.4
